TPU v7x, 256 devices: a whole 4x4x8 slice. The times are simulated.
256 devices in a mesh: seq: 32 (over x, y, core), head: 8 (over z).
Axes of the slice: x: 4, y: 4, z: 8, core: 2. Of those that a mesh axis runs over, the one named last changes fastest.
Arguments:
- new_states: bfloat16 [96, 1024], replicated, may hold values from -6 to 6
- lengths: int32 [24], replicated, may hold values from 1 to 16380, as said below
- cache_keys: bfloat16 [24, 16384, 1024], P(None, 'seq', 'head'), may hold values from -3000 to 3000
- cache_values: bfloat16 [24, 16384, 1024], P(None, 'seq', 'head'), may hold values from -6 to 6
- buckets: int32 [24, 4, 16384], P(None, None, 'seq'), may hold values from 0 to 31, as said below
- attn_gain: float32 [1024], replicated, may hold values from 0.25 to 1.75
- w_query: bfloat16 [1024, 1024], P(None, 'head'), may hold values from -0.0234375 to 0.0234375
- w_key: bfloat16 [1024, 1024], P(None, 'head'), may hold values from -0.1875 to 0.1875
- w_value: bfloat16 [1024, 1024], P(None, 'head'), may hold values from -0.1875 to 0.1875
- rel_bias: float32 [32, 16], P(None, 'head'), may hold values from -27 to 2
- w_out: bfloat16 [1024, 1024], P('head'), may hold values from -0.1875 to 0.1875
- ffn_gain: float32 [1024], replicated, may hold values from 0.25 to 1.75
- w_router: float32 [1024, 16], replicated, may hold values from -0.1875 to 0.1875
- w_gate: bfloat16 [16, 1024, 2816], P('head', None, 'seq'), may hold values from -0.1875 to 0.1875
- w_up: bfloat16 [16, 1024, 2816], P('head', None, 'seq'), may hold values from -0.1875 to 0.1875
- w_down: bfloat16 [16, 2816, 1024], P('head', 'seq'), may hold values from -0.109375 to 0.109375
- expert_picks: int32 [4, 24, 2], replicated, may hold values from 0 to 15, all different within a row; in each aligned block of 24 rows (0 to 23, 24 to 47, ..., all dimensions but the last counted through in order) at most 4 rows name the same one
- final_gain: float32 [1024], replicated, may hold values from 0.25 to 1.75
- w_vocab: bfloat16 [1024, 32128], P(None, 'seq'), may hold values from -0.5 to 0.5
Outputs:
- final_hidden: bfloat16 [96, 1024], P('head')
- hidden_norm: float32 [96], P('head')
- logit_max: float32 [96], P('head')
Inputs may be any that keep to these rules, and one draw needn't show every extreme that they name: `lengths`: some request has exactly 16380 cached positions. buckets[r, t, p] is the T5 relative position bucket (16 exact buckets, then logarithmic up to a distance of 128) of the distance lengths[r] + t - p where that is not negative, else 0. `expert_picks`: A request's two picks at a step differ; at each step no expert is picked by more than 4 requests, a bound that some block reaches.
All inputs are finite; a program needn't handle non-finite values.
Results may differ from a plain program's by a relative error of at most 0.0096.
Values may be sent and summed in bfloat16 or wider, within the bound.
A program may use at most 64 MiB of HBM per device.

v0:
```python
import jax
import jax.numpy as jnp
from jax import lax
from jax.sharding import PartitionSpec as P

CAP = 4


def joined(part, axis, combine):
    gathered = jax.tree.map(lambda a: lax.all_gather(a, axis), part)

    def take(source):
        return jax.tree.map(lambda a: lax.dynamic_index_in_dim(a, source, 0, False), gathered)

    return lax.fori_loop(
        1, lax.axis_size(axis), lambda source, state: combine(state, take(source)), take(0)
    )


def norm_parts(values, gain_row):
    norm_root = jnp.sqrt(jnp.mean(values * values, axis=-1, keepdims=True) + 1e-06)
    return (values / norm_root * gain_row, norm_root[..., 0])


def join_three(earlier_part, later_part):
    joint_top = jnp.maximum(earlier_part[0], later_part[0])
    lead_scale = jnp.exp(earlier_part[0] - joint_top)
    trail_scale = jnp.exp(later_part[0] - joint_top)
    mass = earlier_part[1] * lead_scale + later_part[1] * trail_scale
    weighted = earlier_part[2] * lead_scale[..., None] + later_part[2] * trail_scale[..., None]
    return (joint_top, mass, weighted)


def shards(
    new_states,
    lengths,
    cache_keys,
    cache_values,
    buckets,
    attn_gain,
    w_query,
    w_key,
    w_value,
    rel_bias,
    w_out,
    ffn_gain,
    w_router,
    w_gate,
    w_up,
    w_down,
    expert_picks,
    final_gain,
    w_vocab,
):
    seq_count = lax.axis_size("seq")
    head_count = lax.axis_size("head")
    seq_index = lax.axis_index("seq")
    head_index = lax.axis_index("head")
    requests, span_local, inner_local = cache_keys.shape
    tokens = new_states.shape[0]
    step_count = tokens // requests
    bucket_count, heads_local = rel_bias.shape
    head_dim = inner_local // heads_local
    states = new_states.astype(jnp.float32)
    scaled, _ = norm_parts(states, attn_gain)
    scaled = scaled.astype(jnp.bfloat16)
    queries = (
        jnp.dot(scaled, w_query, preferred_element_type=jnp.float32)
        .astype(jnp.bfloat16)
        .reshape(requests, step_count, heads_local, head_dim)
    )
    key_new = (
        jnp.dot(scaled, w_key, preferred_element_type=jnp.float32)
        .astype(jnp.bfloat16)
        .reshape(requests, step_count, inner_local)
    )
    value_new = (
        jnp.dot(scaled, w_value, preferred_element_type=jnp.float32)
        .astype(jnp.bfloat16)
        .reshape(requests, step_count, inner_local)
    )
    position = seq_index * span_local + jnp.arange(span_local, dtype=jnp.int32)
    target = lengths[:, None] + jnp.arange(step_count, dtype=jnp.int32)[None, :]
    landing = position[None, None, :] == target[:, :, None]
    landed = jnp.any(landing, axis=1)[:, :, None]
    landing_low = landing.astype(jnp.bfloat16)
    placed_keys = jnp.einsum(
        "rtp,rtc->rpc", landing_low, key_new, preferred_element_type=jnp.float32
    ).astype(jnp.bfloat16)
    placed_values = jnp.einsum(
        "rtp,rtc->rpc", landing_low, value_new, preferred_element_type=jnp.float32
    ).astype(jnp.bfloat16)
    key_rows = jnp.where(landed, placed_keys, cache_keys).reshape(
        requests, span_local, heads_local, head_dim
    )
    value_rows = jnp.where(landed, placed_values, cache_values).reshape(
        requests, span_local, heads_local, head_dim
    )
    scores = jnp.einsum("rthd,rphd->rthp", queries, key_rows, preferred_element_type=jnp.float32)
    bucket_hot = (buckets[..., None] == jnp.arange(bucket_count, dtype=jnp.int32)).astype(
        jnp.float32
    )
    scores = scores + jnp.einsum(
        "rtpb,bh->rthp", bucket_hot, rel_bias, precision=lax.Precision.HIGHEST
    )
    allowed = (position[None, None, :] <= target[:, :, None])[:, :, None, :]
    scores = jnp.where(allowed, scores, -1e30)
    local_top = jnp.max(scores, axis=-1)
    weights = jnp.where(allowed, jnp.exp(scores - local_top[..., None]), 0.0)
    local_mass = jnp.sum(weights, axis=-1)
    partial_value = jnp.einsum(
        "rthp,rphd->rthd", weights, value_rows.astype(jnp.float32), precision=lax.Precision.HIGHEST
    )
    out_rows = w_out.astype(jnp.float32)
    global_top, global_mass, summed = joined(
        (local_top, local_mass, partial_value), "seq", join_three
    )
    heads_out = (summed / global_mass[..., None]).reshape(tokens, inner_local)
    projected = jnp.dot(heads_out, out_rows, precision=lax.Precision.HIGHEST)
    mixed_rows = lax.psum(projected, "head")
    hidden_one = states + mixed_rows
    normed, _ = norm_parts(hidden_one, ffn_gain)
    router_logits = jnp.dot(normed, w_router, precision=lax.Precision.HIGHEST)
    normed_low = normed.astype(jnp.bfloat16)
    expert_total = w_router.shape[1]
    local_experts, model_width, units_local = w_gate.shape
    expert_ids = jnp.arange(expert_total, dtype=jnp.int32)
    pick_marks = (expert_picks[..., None] == expert_ids).astype(jnp.int32)
    per_step = jnp.sum(pick_marks, axis=2)
    earlier = jnp.cumsum(per_step, axis=1) - per_step
    slot_index = jnp.sum(pick_marks * earlier[:, :, None, :], axis=-1)
    pick_total = expert_picks.shape[2]
    token_picks = jnp.transpose(expert_picks, (1, 0, 2)).reshape(tokens, pick_total)
    token_slots = jnp.transpose(slot_index, (1, 0, 2)).reshape(tokens, pick_total)
    token_steps = jnp.arange(tokens, dtype=jnp.int32) % step_count
    picked = jnp.sum(
        jnp.where(token_picks[..., None] == expert_ids, router_logits[:, None, :], 0.0), axis=-1
    )
    gate_first = jax.nn.sigmoid(picked[:, 0] - picked[:, 1])
    gate_second = jax.nn.sigmoid(picked[:, 1] - picked[:, 0])
    slot_rows = step_count * CAP
    row_ids = jnp.arange(local_experts * slot_rows, dtype=jnp.int32)
    row_expert = head_index * local_experts + row_ids // slot_rows
    row_step = row_ids // CAP % step_count
    row_slot = row_ids % CAP
    chooser = jnp.zeros((row_ids.shape[0], tokens), jnp.float32)
    for pick_rank in range(pick_total):
        matched = (
            (row_expert[:, None] == token_picks[None, :, pick_rank])
            & (row_step[:, None] == token_steps[None, :])
            & (row_slot[:, None] == token_slots[None, :, pick_rank])
        )
        chooser = chooser + matched.astype(jnp.float32)
    routed = jnp.dot(
        chooser.astype(jnp.bfloat16), normed_low, preferred_element_type=jnp.float32
    ).astype(jnp.bfloat16)
    routed = routed.reshape(local_experts, slot_rows, model_width)
    gate_part = jnp.einsum("esd,edf->esf", routed, w_gate, preferred_element_type=jnp.float32)
    up_part = jnp.einsum("esd,edf->esf", routed, w_up, preferred_element_type=jnp.float32)
    hidden_units = (jax.nn.gelu(gate_part, approximate=True) * up_part).astype(jnp.bfloat16)
    down_part = jnp.einsum("esf,efd->esd", hidden_units, w_down, preferred_element_type=jnp.float32)
    expert_share = lax.psum_scatter(down_part, "seq", scatter_dimension=2, tiled=True).astype(
        jnp.bfloat16
    )
    share_width = expert_share.shape[2]
    collected = lax.all_gather(expert_share[None], ("seq", "head"), axis=0, tiled=True)
    arranged = collected.reshape(seq_count, head_count, local_experts, slot_rows, share_width)
    arranged = jnp.transpose(arranged, (1, 2, 3, 0, 4)).reshape(
        expert_total * slot_rows, seq_count * share_width
    )
    group_size = tokens // head_count
    first_row = head_index * group_size
    own_picks = lax.dynamic_slice_in_dim(token_picks, first_row, group_size, 0)
    own_slots = lax.dynamic_slice_in_dim(token_slots, first_row, group_size, 0)
    own_steps = lax.dynamic_slice_in_dim(token_steps, first_row, group_size, 0)
    own_first = lax.dynamic_slice_in_dim(gate_first, first_row, group_size, 0)
    own_second = lax.dynamic_slice_in_dim(gate_second, first_row, group_size, 0)
    own_hidden = lax.dynamic_slice_in_dim(hidden_one, first_row, group_size, 0)
    flat_rows = own_picks * slot_rows + own_steps[:, None] * CAP + own_slots
    every_row = jnp.arange(expert_total * slot_rows, dtype=jnp.int32)
    select_first = (flat_rows[:, 0:1] == every_row[None, :]).astype(jnp.bfloat16)
    select_second = (flat_rows[:, 1:2] == every_row[None, :]).astype(jnp.bfloat16)
    expert_mix = own_first[:, None] * jnp.dot(
        select_first, arranged, preferred_element_type=jnp.float32
    )
    expert_mix = expert_mix + own_second[:, None] * jnp.dot(
        select_second, arranged, preferred_element_type=jnp.float32
    )
    final_rows = (own_hidden + expert_mix).astype(jnp.bfloat16)
    scaled_out, norm_root = norm_parts(final_rows.astype(jnp.float32), final_gain)
    logits = jnp.dot(scaled_out.astype(jnp.bfloat16), w_vocab, preferred_element_type=jnp.float32)
    top_logit = lax.pmax(jnp.max(logits, axis=-1), "seq")
    return (final_rows, norm_root, top_logit)


def solution(mesh):
    placed = (
        P(),
        P(),
        P(None, "seq", "head"),
        P(None, "seq", "head"),
        P(None, None, "seq"),
        P(),
        P(None, "head"),
        P(None, "head"),
        P(None, "head"),
        P(None, "head"),
        P("head", None),
        P(),
        P(),
        P("head", None, "seq"),
        P("head", None, "seq"),
        P("head", "seq", None),
        P(),
        P(),
        P(None, "seq"),
    )
    return jax.shard_map(
        shards,
        mesh=mesh,
        in_specs=placed,
        out_specs=(P("head", None), P("head"), P("head")),
        check_vma=False,
    )
```

profile of v0, /device:TPU:32, one launch (start us, length us, event | category | flops | bytes accessed | tf_op | source)
XLA Modules:
  0.0 482.6 jit_solution(6117893066806250847)
XLA Ops:
  7.3 1.2 fusion.13
  9.2 1.3 convolution_convert_fusion.2
  10.7 1.3 convolution_convert_fusion.1
  12.3 4.6 copy.74
  17.0 4.7 copy.77
  22.0 2.0 fusion.4
  24.0 3.1 convert_select_fusion.1
  27.1 1.0 convert_select_fusion
  28.8 3.3 convolution_bitcast_fusion.1
  33.2 25.3 %all-gather.1 = f32[768,4,2]{1,2,0:T(2,128)S(1)} all-gather(f32[24,4,2]{1,2,0:T(2,128)S(1)} %fusion.16), channel_id=3, replica_groups=mesh['seq'=32,'head'=8] {'seq'}, dimensions={0}, use_global_device_ids=true | all-gather | bytes 25344 | tf_op jit(solution)/shard_map/all_gather | solution.py:10
  59.2 25.2 %all-gather = f32[768,4,2]{1,2,0:T(2,128)S(1)} all-gather(f32[24,4,2]{1,2,0:T(2,128)S(1)} %get-tuple-element.240), channel_id=2, replica_groups=mesh['seq'=32,'head'=8] {'seq'}, dimensions={0}, use_global_device_ids=true | all-gather | bytes 25344 | tf_op jit(solution)/shard_map/all_gather | solution.py:10
  84.4 1.2 copy.83
  87.0 76.0 %while.19 = (s32[]{:T(128)}, f32[24,4,2]{0,2,1:T(2,128)S(1)}, f32[24,4,2]{0,2,1:T(2,128)S(1)}, f32[24,4,2,64]{3,2,1,0:T(2,128)S(1)}, f32[32,24,4,2]{1,3,2,0:T(2,...) while((s32[]{:T(128)}, f32[24,4,2]{0,2,1:T(2,128)S(1)}, ...), condition=%wide.region_5.6_spmd, body=%wide.region_4.5_spmd.sunk | while | flops 38021 | bytes 256655 | solution.py:15
  87.9 0.9 constant_dynamic-slice_fusion.6
  90.4 0.9 constant_dynamic-slice_fusion.6
  92.8 0.9 constant_dynamic-slice_fusion.6
  95.3 0.9 constant_dynamic-slice_fusion.6
  97.7 0.9 constant_dynamic-slice_fusion.6
  100.2 0.9 constant_dynamic-slice_fusion.6
  102.6 0.9 constant_dynamic-slice_fusion.6
  105.1 0.9 constant_dynamic-slice_fusion.6
  107.6 0.9 constant_dynamic-slice_fusion.6
  110.0 0.9 constant_dynamic-slice_fusion.6
  112.5 0.9 constant_dynamic-slice_fusion.6
  114.9 0.9 constant_dynamic-slice_fusion.6
  117.4 0.9 constant_dynamic-slice_fusion.6
  119.8 0.9 constant_dynamic-slice_fusion.6
  122.3 0.9 constant_dynamic-slice_fusion.6
  124.7 0.9 constant_dynamic-slice_fusion.6
  127.2 0.9 constant_dynamic-slice_fusion.6
  129.6 0.9 constant_dynamic-slice_fusion.6
  132.1 0.9 constant_dynamic-slice_fusion.6
  134.5 0.9 constant_dynamic-slice_fusion.6
  137.0 0.9 constant_dynamic-slice_fusion.6
  151.7 0.9 constant_dynamic-slice_fusion.6
  156.6 0.9 constant_dynamic-slice_fusion.6
  163.4 1.1 fusion.77
  164.6 72.5 %all-reduce.2.cloned.1.call-done = f32[96,1024]{1,0:T(8,128)} async-done(((f32[96,1024]{1,0:T(8,128)}), f32[96,1024]{1,0:T(8,128)}) %all-reduce.2.cloned.1.call-update) | async-done | bytes 393232 | tf_op jit(solution)/shard_map/psum | solution.py:120
  237.1 1.1 multiply_reduce_fusion
  239.1 1.2 fusion.78
  240.3 2.0 fusion.12
  242.3 1.3 copy.98
  243.6 1.4 reshape.208
  245.2 83.7 %reduce-scatter.4.cloned.1.call-done = f32[32,32]{1,0:T(8,128)} async-done(((f32[1024,32]{1,0:T(8,128)}), f32[32,32]{1,0:T(8,128)}) %reduce-scatter.4.cloned.1.call-update) | async-done | bytes 4112
  329.8 73.4 %all-gather.3 = bf16[512,16,32]{2,1,0:T(8,128)(2,1)S(1)} all-gather(bf16[2,16,32]{2,1,0:T(8,128)(2,1)S(1)} %copy.99), channel_id=5, replica_groups=mesh['seq'=32,'head'=8] {'seq','head'}, dimensions={0}, use_global_device_ids=true | all-gather | bytes 526336 | tf_op jit(solution)/shard_map/all_gather | solution.py:166
  403.2 2.7 copy.112
  405.9 3.5 reshape.189
  410.8 65.3 %pmax.7 = f32[12]{0:T(128)} all-reduce(f32[12]{0:T(128)S(1)} %convolution_reduce_fusion), channel_id=1, replica_groups=mesh['seq'=32,'head'=8] {'seq'}, use_global_device_ids=true, to_apply=%region_15.16 | all-reduce | flops 12 | bytes 96 | tf_op jit(solution)/shard_map/pmax | solution.py:192
  (217 shorter events, 63.7 us)
Async XLA Ops:
  7.2 402.9 %copy-start = (bf16[1024,1004]{0,1:T(8,128)(2,1)S(1)}, bf16[1024,1004]{0,1:T(8,128)(2,1)}, u32[]{:S(2)}) copy-start(bf16[1024,1004]{0,1:T(8,128)(2,1)} %param.39) | copy-start | bytes 6168580
  7.2 4.8 copy-start.2
  7.2 4.8 copy-start.12
  7.2 4.8 copy-start.9
  7.2 78.8 %all-gather.6.cloned.1.call-start = ((), (), s32[]{:S(2)}) async-start(), calls=%async_computation.2 | async-start | bytes 3244032 | tf_op jit(solution)/shard_map/all_gather | solution.py:10
  16.9 5.0 %copy-start.10 = (s32[24,4,512]{2,1,0:T(4,128)S(1)}, s32[24,4,512]{2,1,0:T(4,128)}, u32[]{:S(2)}) copy-start(s32[24,4,512]{2,1,0:T(4,128)} %param.25) | copy-start | bytes 589828
  17.0 5.0 %copy-start.14 = (f32[32,2]{0,1:T(2,128)S(1)}, f32[32,2]{0,1:T(2,128)}, u32[]{:S(2)}) copy-start(f32[32,2]{0,1:T(2,128)} %param.30) | copy-start | bytes 772
  24.0 3.1 copy-start.1
  28.8 3.3 copy-start.6
  32.1 205.0 %all-reduce.2.cloned.1.call-start = ((), (), s32[]{:S(2)}) async-start(), calls=%async_computation.1 | async-start | bytes 786432 | tf_op jit(solution)/shard_map/psum | solution.py:120
  59.1 104.3 %copy-start.4 = (bf16[128,1024]{1,0:T(8,128)(2,1)S(1)}, bf16[128,1024]{1,0:T(8,128)(2,1)}, u32[]{:S(2)}) copy-start(bf16[128,1024]{1,0:T(8,128)(2,1)} %param.31) | copy-start | bytes 786436
  86.9 151.3 %copy-start.11 = (f32[1024,16]{0,1:T(8,128)S(1)}, f32[1024,16]{0,1:T(8,128)}, u32[]{:S(2)}) copy-start(f32[1024,16]{0,1:T(8,128)} %param.33) | copy-start | bytes 196612
  87.0 151.3 %copy-start.13 = (f32[1024]{0:T(1024)S(1)}, f32[1024]{0:T(1024)}, u32[]{:S(2)}) copy-start(f32[1024]{0:T(1024)} %param.32) | copy-start | bytes 12292
  163.0 77.3 %copy-start.3 = (bf16[2,88,1024]{2,1,0:T(8,128)(2,1)S(1)}, bf16[2,88,1024]{2,1,0:T(8,128)(2,1)}, u32[]{:S(2)}) copy-start(bf16[2,88,1024]{2,1,0:T(8,128)(2,1)} %param.36) | copy-start | bytes 1081348
  164.5 164.3 %reduce-scatter.4.cloned.1.call-start = ((), (), s32[]{:S(2)}) async-start(), calls=%async_computation.3 | async-start | bytes 540672
  403.2 6.8 %copy-start.7 = (f32[1024]{0:T(1024)S(1)}, f32[1024]{0:T(1024)}, u32[]{:S(2)}) copy-start(f32[1024]{0:T(1024)} %param.38) | copy-start | bytes 12292
  410.0 66.1 %copy-start.5 = (bf16[12,1024]{1,0:T(8,128)(2,1)}, bf16[12,1024]{1,0:T(8,128)(2,1)S(1)}, u32[]{:S(2)}) copy-start(bf16[12,1024]{1,0:T(8,128)(2,1)S(1)} %get-tuple-element.243) | copy-start | bytes 73732
  410.0 66.1 %copy-start.8 = (f32[12]{0:T(128)}, f32[12]{0:T(128)S(1)}, u32[]{:S(2)}) copy-start(f32[12]{0:T(128)S(1)} %add_sqrt_fusion) | copy-start | bytes 148
Sparse Core Ops, SparseCore 0:
  32.2 53.7 all-gather.5
  164.6 72.4 all-reduce.1
  245.2 83.6 reduce-scatter.3
where the time goes:
time: 485 us; the launch traced here: 483 us
  blocking collectives  189 us (39%)
  waiting for transfers between devices  156 us (32%)
  local copies, waits for them, and re-layouts  58.1 us (12%)
  other arithmetic  44.9 us (9%)
  matrix products  19.3 us (4%)
  between operations  14.1 us (3%)
    unnamed x4, waiting for transfers between devices  83.7 us
    all_gather x1, blocking collectives, shards(): lax.all_gather(expert_share[None], ('seq', 'head'), axis=0, tiled=True)  73.4 us
    psum x1, waiting for transfers between devices, shards(): mixed_rows = lax.psum(projected, 'head')  72.5 us
    pmax x1, blocking collectives, shards(): top_logit = lax.pmax(jnp.max(logits, axis=-1), 'seq')  65.3 us
    all_gather x2, blocking collectives, joined(): gathered = jax.tree.map(lambda a: lax.all_gather(a, axis), part)  50.5 us
    dynamic_slice x34, local copies, waits for them, and re-layouts, take(): lax.dynamic_index_in_dim(a, source, 0, False)  28.9 us
    add x31, other arithmetic, join_three(): mass = earlier_part[1] * lead_scale + later_part[1] * trail_scale  21.9 us
    add x31, other arithmetic, join_three(): earlier_part[2] * lead_scale[..., None]  18.8 us
  transfers between devices with their start and end apart: 3, of which 3 were waited for; matrix products, arithmetic and copies ran while one was open for 1% of the time, Pallas kernels for 0%

commit v1 on v0

--- a/solution.py
+++ b/solution.py
@@ -117,7 +117,11 @@
     )
     heads_out = (summed / global_mass[..., None]).reshape(tokens, inner_local)
     projected = jnp.dot(heads_out, out_rows, precision=lax.Precision.HIGHEST)
-    mixed_rows = lax.psum(projected, "head")
+    mixed_rows = projected
+    for hop in (1, 2, 4):
+        mixed_rows = mixed_rows + lax.ppermute(
+            mixed_rows, "head", [(dev, dev ^ hop) for dev in range(8)]
+        )
     hidden_one = states + mixed_rows
     normed, _ = norm_parts(hidden_one, ffn_gain)
     router_logits = jnp.dot(normed, w_router, precision=lax.Precision.HIGHEST)

time: 485 us -> 463 us (0.955)
  waiting for transfers between devices: 156 us -> 128 us
  starting transfers between devices: 0.12 us -> 8.15 us
    psum x1 -> x0, waiting for transfers between devices: 72.5 us -> none  [shards(): mixed_rows = lax.psum(projected, 'head')]
    ppermute x0 -> x3, waiting for transfers between devices: none -> 39.4 us  [shards(): lax.ppermute(mixed_rows, 'head', [(dev, dev ^ hop) for dev in range(8)])]
    ppermute x0 -> x3, starting transfers between devices: none -> 8.07 us  [shards(): lax.ppermute(mixed_rows, 'head', [(dev, dev ^ hop) for dev in range(8)])]
    unnamed x4 -> x3, waiting for transfers between devices: 83.7 us -> 88.2 us
    unnamed x36 -> x38, local copies, waits for them, and re-layouts: 13.1 us -> 13.1 us
  transfers between devices with their start and end apart: 3 -> 5, of which waited for: 3 -> 5; matrix products, arithmetic and copies ran while one was open for 1% -> 1% of each run, Pallas kernels for 0% -> 0%
where the time goes in v1:
time: 463 us; the launch traced here: 460 us
  blocking collectives  189 us (41%)
  waiting for transfers between devices  128 us (28%)
  local copies, waits for them, and re-layouts  58.1 us (13%)
  other arithmetic  44 us (10%)
  matrix products  17.4 us (4%)
  between operations  14.4 us (3%)
  starting transfers between devices  8.15 us (2%)
    unnamed x3, waiting for transfers between devices  88.2 us
    all_gather x1, blocking collectives, shards(): lax.all_gather(expert_share[None], ('seq', 'head'), axis=0, tiled=True)  73.4 us
    pmax x1, blocking collectives, shards(): top_logit = lax.pmax(jnp.max(logits, axis=-1), 'seq')  65.3 us
    all_gather x2, blocking collectives, joined(): gathered = jax.tree.map(lambda a: lax.all_gather(a, axis), part)  50.3 us
    ppermute x3, waiting for transfers between devices, shards(): lax.ppermute(mixed_rows, 'head', [(dev, dev ^ hop) for dev in range(8)])  39.4 us
    dynamic_slice x34, local copies, waits for them, and re-layouts, take(): lax.dynamic_index_in_dim(a, source, 0, False)  28.9 us
    add x31, other arithmetic, join_three(): mass = earlier_part[1] * lead_scale + later_part[1] * trail_scale  21.8 us
    add x31, other arithmetic, join_three(): earlier_part[2] * lead_scale[..., None]  18.8 us
  transfers between devices with their start and end apart: 5, of which 5 were waited for; matrix products, arithmetic and copies ran while one was open for 1% of the time, Pallas kernels for 0%

profile of v1, /device:TPU:32, one launch (start us, length us, event | category | flops | bytes accessed | tf_op | source)
XLA Modules:
  0.0 460.0 jit_solution(9163968570619371912)
XLA Ops:
  7.3 1.2 fusion.11
  9.2 1.3 convolution_convert_fusion.2
  10.7 1.3 convolution_convert_fusion.1
  12.3 4.6 %copy.74 = bf16[24,512,128]{1,2,0:T(8,128)(2,1)} copy(bf16[24,512,128]{2,1,0:T(8,128)(2,1)} %param.23) | data formatting | bytes 6291456 | tf_op args[2]
  17.0 4.7 %copy.77 = bf16[24,512,128]{1,2,0:T(8,128)(2,1)} copy(bf16[24,512,128]{2,1,0:T(8,128)(2,1)} %param.24) | data formatting | bytes 6291456 | tf_op args[3]
  22.0 2.0 fusion.4
  24.0 3.1 convert_select_fusion.1
  27.1 1.0 convert_select_fusion
  28.8 3.3 convolution_bitcast_fusion.1
  32.5 25.2 %all-gather.1 = f32[768,4,2]{1,2,0:T(2,128)S(1)} all-gather(f32[24,4,2]{1,2,0:T(2,128)S(1)} %fusion.14), channel_id=3, replica_groups=mesh['seq'=32,'head'=8] {'seq'}, dimensions={0}, use_global_device_ids=true | all-gather | bytes 25344 | tf_op jit(solution)/shard_map/all_gather | solution.py:10
  58.4 25.1 %all-gather = f32[768,4,2]{1,2,0:T(2,128)S(1)} all-gather(f32[24,4,2]{1,2,0:T(2,128)S(1)} %get-tuple-element.240), channel_id=2, replica_groups=mesh['seq'=32,'head'=8] {'seq'}, dimensions={0}, use_global_device_ids=true | all-gather | bytes 25344 | tf_op jit(solution)/shard_map/all_gather | solution.py:10
  83.6 1.2 copy.83
  86.6 76.0 %while.19 = (s32[]{:T(128)}, f32[24,4,2]{0,2,1:T(2,128)S(1)}, f32[24,4,2]{0,2,1:T(2,128)S(1)}, f32[24,4,2,64]{3,2,1,0:T(2,128)S(1)}, f32[32,24,4,2]{1,3,2,0:T(2,...) while((s32[]{:T(128)}, f32[24,4,2]{0,2,1:T(2,128)S(1)}, ...), condition=%wide.region_5.6_spmd, body=%wide.region_4.5_spmd.sunk | while | flops 38021 | bytes 256655 | solution.py:15
  87.5 0.9 constant_dynamic-slice_fusion.6
  90.0 0.9 constant_dynamic-slice_fusion.6
  92.4 0.9 constant_dynamic-slice_fusion.6
  94.9 0.9 constant_dynamic-slice_fusion.6
  97.3 0.9 constant_dynamic-slice_fusion.6
  99.8 0.9 constant_dynamic-slice_fusion.6
  102.3 0.9 constant_dynamic-slice_fusion.6
  104.7 0.9 constant_dynamic-slice_fusion.6
  107.2 0.9 constant_dynamic-slice_fusion.6
  109.6 0.9 constant_dynamic-slice_fusion.6
  112.1 0.9 constant_dynamic-slice_fusion.6
  114.5 0.9 constant_dynamic-slice_fusion.6
  117.0 0.9 constant_dynamic-slice_fusion.6
  119.4 0.9 constant_dynamic-slice_fusion.6
  121.9 0.9 constant_dynamic-slice_fusion.6
  124.4 0.9 constant_dynamic-slice_fusion.6
  126.8 0.9 constant_dynamic-slice_fusion.6
  129.3 0.9 constant_dynamic-slice_fusion.6
  134.1 0.9 constant_dynamic-slice_fusion.6
  151.3 0.9 constant_dynamic-slice_fusion.6
  161.1 0.9 constant_dynamic-slice_fusion.6
  164.7 10.0 %collective-permute-done = f32[96,1024]{1,0:T(8,128)S(1)} collective-permute-done((f32[96,1024]{1,0:T(8,128)S(1)}, f32[96,1024]{1,0:T(8,128)S(1)}, u32[]{:S(2)}, u32[]{:S(2)}) %collective-permute-start) | collective-permute-done | bytes 393248 | tf_op jit(solution)/shard_map/ppermute | solution.py:122
  174.8 2.2 collective-permute-start.1
  177.2 16.2 %collective-permute-done.1 = f32[96,1024]{1,0:T(8,128)S(1)} collective-permute-done((f32[96,1024]{1,0:T(8,128)S(1)}, f32[96,1024]{1,0:T(8,128)S(1)}, u32[]{:S(2)}, u32[]{:S(2)}) %collective-permute-start.1) | collective-permute-done | bytes 393248 | tf_op jit(solution)/shard_map/ppermute | solution.py:122
  193.4 5.2 %collective-permute-start.2 = (f32[96,1024]{1,0:T(8,128)S(1)}, f32[96,1024]{1,0:T(8,128)S(1)}, u32[]{:S(2)}, u32[]{:S(2)}) collective-permute-start(f32[96,1024]{1,0:T(8,128)S(1)} %add.242), channel_id=1, source_target_pairs={{0,4},{1,5},{2,6},{3,7},{4,0},{5,1},{6,2},{7,3},{8,12},{9,13},{10,... | collective-permute-start | bytes 1179656 | tf_op jit(solution)/shard_map/ppermute | solution.py:122
  198.6 13.2 %collective-permute-done.2 = f32[96,1024]{1,0:T(8,128)S(1)} collective-permute-done((f32[96,1024]{1,0:T(8,128)S(1)}, f32[96,1024]{1,0:T(8,128)S(1)}, u32[]{:S(2)}, u32[]{:S(2)}) %collective-permute-start.2) | collective-permute-done | bytes 393248 | tf_op jit(solution)/shard_map/ppermute | solution.py:122
  212.0 1.3 fusion.29
  213.8 1.0 fusion.10
  214.9 1.3 copy.98
  216.2 1.4 reshape.208
  217.8 88.2 %reduce-scatter.4.cloned.1.call-done = f32[32,32]{1,0:T(8,128)} async-done(((f32[1024,32]{1,0:T(8,128)}), f32[32,32]{1,0:T(8,128)}) %reduce-scatter.4.cloned.1.call-update) | async-done | bytes 4112
  306.9 73.4 %all-gather.3 = bf16[512,16,32]{2,1,0:T(8,128)(2,1)S(1)} all-gather(bf16[2,16,32]{2,1,0:T(8,128)(2,1)S(1)} %copy.99), channel_id=5, replica_groups=mesh['seq'=32,'head'=8] {'seq','head'}, dimensions={0}, use_global_device_ids=true | all-gather | bytes 526336 | tf_op jit(solution)/shard_map/all_gather | solution.py:170
  380.3 2.7 copy.112
  383.0 3.5 reshape.189
  387.9 65.3 %pmax.7 = f32[12]{0:T(128)} all-reduce(f32[12]{0:T(128)S(1)} %convolution_reduce_fusion), channel_id=1, replica_groups=mesh['seq'=32,'head'=8] {'seq'}, use_global_device_ids=true, to_apply=%region_14.15 | all-reduce | flops 12 | bytes 96 | tf_op jit(solution)/shard_map/pmax | solution.py:196
  (224 shorter events, 67.0 us)
Async XLA Ops:
  7.2 379.9 %copy-start = (bf16[1024,1004]{0,1:T(8,128)(2,1)S(1)}, bf16[1024,1004]{0,1:T(8,128)(2,1)}, u32[]{:S(2)}) copy-start(bf16[1024,1004]{0,1:T(8,128)(2,1)} %param.39) | copy-start | bytes 6168580
  7.2 4.8 %copy-start.2 = (bf16[96,1024]{1,0:T(8,128)(2,1)S(1)}, bf16[96,1024]{1,0:T(8,128)(2,1)}, u32[]{:S(2)}) copy-start(bf16[96,1024]{1,0:T(8,128)(2,1)} %param.21) | copy-start | bytes 589828
  7.2 4.8 %copy-start.13 = (f32[1024]{0:T(1024)S(1)}, f32[1024]{0:T(1024)}, u32[]{:S(2)}) copy-start(f32[1024]{0:T(1024)} %param.26) | copy-start | bytes 12292
  7.2 4.8 %copy-start.11 = (bf16[1024,128]{1,0:T(8,128)(2,1)S(1)}, bf16[1024,128]{1,0:T(8,128)(2,1)}, u32[]{:S(2)}) copy-start(bf16[1024,128]{1,0:T(8,128)(2,1)} %param.28) | copy-start | bytes 786436
  7.2 78.4 %all-gather.6.cloned.1.call-start = ((), (), s32[]{:S(2)}) async-start(), calls=%async_computation.1 | async-start | bytes 3244032 | tf_op jit(solution)/shard_map/all_gather | solution.py:10
  16.9 5.0 %copy-start.12 = (s32[24,4,512]{2,1,0:T(4,128)S(1)}, s32[24,4,512]{2,1,0:T(4,128)}, u32[]{:S(2)}) copy-start(s32[24,4,512]{2,1,0:T(4,128)} %param.25) | copy-start | bytes 589828
  17.0 5.0 %copy-start.15 = (f32[32,2]{0,1:T(2,128)S(1)}, f32[32,2]{0,1:T(2,128)}, u32[]{:S(2)}) copy-start(f32[32,2]{0,1:T(2,128)} %param.30) | copy-start | bytes 772
  24.0 3.1 copy-start.1
  32.1 273.9 %reduce-scatter.4.cloned.1.call-start = ((), (), s32[]{:S(2)}) async-start(), calls=%async_computation.2 | async-start | bytes 540672
  58.4 104.7 %copy-start.6 = (bf16[128,1024]{1,0:T(8,128)(2,1)S(1)}, bf16[128,1024]{1,0:T(8,128)(2,1)}, u32[]{:S(2)}) copy-start(bf16[128,1024]{1,0:T(8,128)(2,1)} %param.31) | copy-start | bytes 786436
  83.6 80.4 %copy-start.8 = (s32[4,24,2]{1,2,0:T(2,128)S(1)}, s32[4,24,2]{1,2,0:T(2,128)}, u32[]{:S(2)}) copy-start(s32[4,24,2]{1,2,0:T(2,128)} %param.37) | copy-start | bytes 2308
  162.6 49.4 %copy-start.14 = (f32[1024]{0:T(1024)S(1)}, f32[1024]{0:T(1024)}, u32[]{:S(2)}) copy-start(f32[1024]{0:T(1024)} %param.32) | copy-start | bytes 12292
  163.4 11.3 %collective-permute-start = (f32[96,1024]{1,0:T(8,128)S(1)}, f32[96,1024]{1,0:T(8,128)S(1)}, u32[]{:S(2)}, u32[]{:S(2)}) collective-permute-start(f32[96,1024]{1,0:T(8,128)S(1)} %fusion.75), channel_id=1, source_target_pairs={{0,1},{1,0},{2,3},{3,2},{4,5},{5,4},{6,7},{7,6},{8,9},{9,8},{10,11... | collective-permute-start | bytes 1179656 | tf_op jit(solution)/shard_map/ppermute | solution.py:122
  164.7 48.9 %copy-start.5 = (bf16[2,1024,88]{1,2,0:T(8,128)(2,1)S(1)}, bf16[2,1024,88]{1,2,0:T(8,128)(2,1)}, u32[]{:S(2)}) copy-start(bf16[2,1024,88]{1,2,0:T(8,128)(2,1)} %param.34) | copy-start | bytes 1081348
  174.7 39.1 %copy-start.3 = (bf16[2,88,1024]{2,1,0:T(8,128)(2,1)S(1)}, bf16[2,88,1024]{2,1,0:T(8,128)(2,1)}, u32[]{:S(2)}) copy-start(bf16[2,88,1024]{2,1,0:T(8,128)(2,1)} %param.36) | copy-start | bytes 1081348
  174.8 39.1 %copy-start.4 = (bf16[2,1024,88]{1,2,0:T(8,128)(2,1)S(1)}, bf16[2,1024,88]{1,2,0:T(8,128)(2,1)}, u32[]{:S(2)}) copy-start(bf16[2,1024,88]{1,2,0:T(8,128)(2,1)} %param.35) | copy-start | bytes 1081348
  174.8 18.6 %collective-permute-start.1 = (f32[96,1024]{1,0:T(8,128)S(1)}, f32[96,1024]{1,0:T(8,128)S(1)}, u32[]{:S(2)}, u32[]{:S(2)}) collective-permute-start(f32[96,1024]{1,0:T(8,128)S(1)} %add.241), channel_id=1, source_target_pairs={{0,2},{1,3},{2,0},{3,1},{4,6},{5,7},{6,4},{7,5},{8,10},{9,11},{10,... | collective-permute-start | bytes 1179656 | tf_op jit(solution)/shard_map/ppermute | solution.py:122
  193.4 18.4 %collective-permute-start.2 = (f32[96,1024]{1,0:T(8,128)S(1)}, f32[96,1024]{1,0:T(8,128)S(1)}, u32[]{:S(2)}, u32[]{:S(2)}) collective-permute-start(f32[96,1024]{1,0:T(8,128)S(1)} %add.242), channel_id=1, source_target_pairs={{0,4},{1,5},{2,6},{3,7},{4,0},{5,1},{6,2},{7,3},{8,12},{9,13},{10,... | collective-permute-start | bytes 1179656 | tf_op jit(solution)/shard_map/ppermute | solution.py:122
  380.3 6.8 %copy-start.9 = (f32[1024]{0:T(1024)S(1)}, f32[1024]{0:T(1024)}, u32[]{:S(2)}) copy-start(f32[1024]{0:T(1024)} %param.38) | copy-start | bytes 12292
  387.1 66.1 %copy-start.7 = (bf16[12,1024]{1,0:T(8,128)(2,1)}, bf16[12,1024]{1,0:T(8,128)(2,1)S(1)}, u32[]{:S(2)}) copy-start(bf16[12,1024]{1,0:T(8,128)(2,1)S(1)} %get-tuple-element.243) | copy-start | bytes 73732
  387.1 66.1 %copy-start.10 = (f32[12]{0:T(128)}, f32[12]{0:T(128)S(1)}, u32[]{:S(2)}) copy-start(f32[12]{0:T(128)S(1)} %add_sqrt_fusion) | copy-start | bytes 148
Sparse Core Ops, SparseCore 0:
  32.2 53.4 all-gather.5
  217.7 88.1 reduce-scatter.3
